TPU v7x, 32 devices: a whole 2x2x4 slice. The times are simulated.
32 devices in a mesh: dp: 8 (over z, x), space: 4 (over y, core).
Axes of the slice: x: 2, y: 2, z: 4, core: 2. Of those that a mesh axis runs over, the one named last changes fastest.
Arguments:
- latents: bfloat16 [48, 8, 32, 1280], P('dp', 'space'), may hold values from -42 to 42
- buckets: int32 [48, 2], P('dp'), may hold values from 6 to 32, as said below
- gn_gain: float32 [1280], replicated, may hold values from 0.1 to 1.9
- gn_shift: float32 [1280], replicated, may hold values from -3 to 3
- conv_weight: bfloat16 [9, 1280, 1280], P(None, 'dp'), may hold values from -0.0546875 to 0.0546875
- time_bias: float32 [48, 1280], P('dp'), may hold values from -5 to 5
Outputs:
- result: bfloat16 [48, 8, 32, 1280], P('dp', 'space')
Inputs may be any that keep to these rules, and one draw needn't show every extreme that they name: `buckets`: column 0 is a frame's height, column 1 its width; heights are at least 6 and at most 8, widths at least 24 and at most 32; in every draw some frame has height 8 and width 32.
All inputs are finite; a program needn't handle non-finite values.
Results may differ from a plain program's by a relative error of at most 0.0035.
Values may be sent and summed in bfloat16 or wider, within the bound.
No kernel may reach another device: no remote copies, remote signals or barrier semaphores. Data moves between devices by JAX's collectives and lax.ppermute only.
A program may use at most 64 MiB of HBM per device.

v0:
```python
import jax
import jax.numpy as jnp
from jax import lax
from jax.sharding import PartitionSpec as P

GROUPS = 32
eps = 1e-05


def with_halo(x, sides, width):
    for axis, dim in sides:
        size, length = (lax.axis_size(axis), x.shape[dim])
        up = [(i, (i + 1) % size) for i in range(size - 1)]
        down = [(j, i) for i, j in up]
        last = lax.slice_in_dim(x, length - width, length, axis=dim)
        first = lax.slice_in_dim(x, 0, width, axis=dim)
        before = lax.ppermute(last, axis, up)
        after = lax.ppermute(first, axis, down)
        x = jnp.concatenate([before, x, after], axis=dim)
    return x


def tap_product(window, panel):
    return lax.dot_general(
        window, panel, (((3,), (1,)), ((), ())), preferred_element_type=jnp.float32
    )


def on_device(latents, buckets, gn_gain, gn_shift, conv_weight, time_bias):
    frames, rows, cols, chans = latents.shape
    members = chans // GROUPS
    row_ids = lax.axis_index("space") * rows + jnp.arange(rows, dtype=jnp.int32)
    col_ids = jnp.arange(cols, dtype=jnp.int32)
    valid = (
        (row_ids[None, :, None] < buckets[:, 0][:, None, None])
        & (col_ids[None, None, :] < buckets[:, 1][:, None, None])
    ).astype(jnp.float32)
    count = (buckets[:, 0] * buckets[:, 1]).astype(jnp.float32)[:, None] * members
    values = latents.astype(jnp.float32).reshape(frames, rows, cols, GROUPS, members)
    weight_mask = valid[:, :, :, None, None]
    total = lax.psum(jnp.sum(values * weight_mask, axis=(1, 2, 4)), "space")
    mean = total / count
    centered = values - mean[:, None, None, :, None]
    spread = lax.psum(jnp.sum(centered * centered * weight_mask, axis=(1, 2, 4)), "space") / count
    normed = (centered / jnp.sqrt(spread[:, None, None, :, None] + eps)).reshape(
        frames, rows, cols, chans
    )
    normed = normed * gn_gain + gn_shift
    act = (valid[..., None] * jax.nn.silu(normed)).astype(jnp.bfloat16)
    extended = with_halo(act, (("space", 1),), 1)
    padded = jnp.pad(extended, ((0, 0), (0, 0), (1, 1), (0, 0)))

    def add_tap(index, accum):
        window = lax.dynamic_slice(
            padded, (0, index // 3, index % 3, 0), (frames, rows, cols, chans)
        )
        panel = lax.dynamic_index_in_dim(conv_weight, index, 0, keepdims=False)
        return accum + tap_product(window, lax.all_gather(panel, "dp", axis=0, tiled=True))

    conv = lax.fori_loop(0, 9, add_tap, jnp.zeros((frames, rows, cols, chans), jnp.float32))
    conv_out = conv.astype(jnp.bfloat16)
    summed = latents.astype(jnp.float32) + valid[..., None] * (
        conv_out.astype(jnp.float32) + time_bias[:, None, None, :]
    )
    return summed.astype(jnp.bfloat16)


def solution(mesh):
    in_specs = (
        P("dp", "space", None, None),
        P("dp", None),
        P(),
        P(),
        P(None, "dp", None),
        P("dp", None),
    )
    out_specs = P("dp", "space", None, None)
    return jax.shard_map(
        on_device, mesh=mesh, in_specs=in_specs, out_specs=out_specs, check_vma=False
    )
```

profile of v0, /device:TPU:0, one launch (start us, length us, event | category | flops | bytes accessed | tf_op | source)
XLA Modules:
  0.0 674.8 jit_solution(2371292868569001316)
XLA Ops:
  6.5 0.8 multiply_bitcast_fusion
  7.3 0.8 slice_bitcast_fusion.1
  8.1 0.1 iota_compare_fusion.2
  8.2 0.1 broadcast_compare_fusion
  8.2 0.1 and_convert_fusion
  8.3 1.6 fusion.19
  9.9 0.1 reduce_sum.24
  10.0 0.1 reduce_sum.25
  10.1 8.4 %psum.14 = f32[6,32]{1,0:T(8,128)S(1)} all-reduce(f32[6,32]{1,0:T(8,128)S(1)} %reduce_sum.25), channel_id=1, replica_groups=mesh['dp'=8,'space'=4] {'space'}, use_global_device_ids=true, to_apply=%region_2.0 | all-reduce | flops 192 | bytes 1536 | tf_op jit(solution)/shard_map/psum | solution.py:41
  18.5 0.1 broadcast_divide_fusion
  18.6 0.1 sub.20
  18.6 0.1 sub.21
  18.8 0.5 fusion.16
  19.3 0.1 reduce_sum.36
  19.4 0.1 reduce_sum.37
  19.5 5.8 psum.15
  25.3 0.1 add_sqrt_fusion
  25.3 0.1 div.48
  25.4 0.1 div.49
  25.6 0.8 multiply_convert_fusion
  26.4 0.8 fusion.21
  27.2 1.7 collective-permute-start
  28.9 1.3 collective-permute-start.1
  30.2 0.3 collective-permute-done
  30.6 2.2 collective-permute-done.1
  32.8 1.9 fusion.12
  34.7 630.7 %while.16 = (s32[]{:T(128)}, f32[6,2,32,1280]{3,2,1,0:T(8,128)}, bf16[6,4,34,1280]{3,2,1,0:T(8,128)(2,1)}, bf16[9,160,1280]{2,1,0:T(8,128)(2,1)}, s32[]{:T(128)}...) while((s32[]{:T(128)}, f32[6,2,32,1280]{3,2,1,0:T(8,128)}, ...), condition=%wide.region_7.8_spmd.clone, body=%wide.region_6.7_spmd.clone.sunk | while | flops 1259274240 | bytes 20070744 | solution.py:60
  34.7 1.8 constant_dynamic-slice_fusion.2
  36.5 0.0 all-gather.6.cloned.1.call-update
  36.6 70.1 %all-gather.6.cloned.1.call-done = bf16[1,1280,1280]{2,1,0:T(8,128)(2,1)} async-done(((bf16[1,160,1280]{2,1,0:T(8,128)(2,1)}), bf16[1,1280,1280]{2,1,0:T(8,128)(2,1)}) %all-gather.6.cloned.1.call-update) | async-done | bytes 3276816 | tf_op jit(solution)/shard_map/while/body/eval_jaxpr/all_gather | solution.py:58
  106.7 5.1 fusion.27
  111.8 1.8 constant_dynamic-slice_fusion.2
  113.6 0.0 all-gather.6.cloned.1.call-update
  113.6 61.7 %all-gather.6.cloned.1.call-done = bf16[1,1280,1280]{2,1,0:T(8,128)(2,1)} async-done(((bf16[1,160,1280]{2,1,0:T(8,128)(2,1)}), bf16[1,1280,1280]{2,1,0:T(8,128)(2,1)}) %all-gather.6.cloned.1.call-update) | async-done | bytes 3276816 | tf_op jit(solution)/shard_map/while/body/eval_jaxpr/all_gather | solution.py:58
  175.4 5.7 fusion.27
  181.1 1.8 constant_dynamic-slice_fusion.2
  182.9 0.0 all-gather.6.cloned.1.call-update
  182.9 61.7 %all-gather.6.cloned.1.call-done = bf16[1,1280,1280]{2,1,0:T(8,128)(2,1)} async-done(((bf16[1,160,1280]{2,1,0:T(8,128)(2,1)}), bf16[1,1280,1280]{2,1,0:T(8,128)(2,1)}) %all-gather.6.cloned.1.call-update) | async-done | bytes 3276816 | tf_op jit(solution)/shard_map/while/body/eval_jaxpr/all_gather | solution.py:58
  244.7 5.7 fusion.27
  250.4 1.8 constant_dynamic-slice_fusion.2
  252.2 0.0 all-gather.6.cloned.1.call-update
  252.2 61.4 %all-gather.6.cloned.1.call-done = bf16[1,1280,1280]{2,1,0:T(8,128)(2,1)} async-done(((bf16[1,160,1280]{2,1,0:T(8,128)(2,1)}), bf16[1,1280,1280]{2,1,0:T(8,128)(2,1)}) %all-gather.6.cloned.1.call-update) | async-done | bytes 3276816 | tf_op jit(solution)/shard_map/while/body/eval_jaxpr/all_gather | solution.py:58
  313.7 5.7 fusion.27
  319.4 1.8 constant_dynamic-slice_fusion.2
  321.2 0.0 all-gather.6.cloned.1.call-update
  321.3 61.4 %all-gather.6.cloned.1.call-done = bf16[1,1280,1280]{2,1,0:T(8,128)(2,1)} async-done(((bf16[1,160,1280]{2,1,0:T(8,128)(2,1)}), bf16[1,1280,1280]{2,1,0:T(8,128)(2,1)}) %all-gather.6.cloned.1.call-update) | async-done | bytes 3276816 | tf_op jit(solution)/shard_map/while/body/eval_jaxpr/all_gather | solution.py:58
  382.7 5.7 fusion.27
  388.4 1.8 constant_dynamic-slice_fusion.2
  390.2 0.0 all-gather.6.cloned.1.call-update
  390.3 61.4 %all-gather.6.cloned.1.call-done = bf16[1,1280,1280]{2,1,0:T(8,128)(2,1)} async-done(((bf16[1,160,1280]{2,1,0:T(8,128)(2,1)}), bf16[1,1280,1280]{2,1,0:T(8,128)(2,1)}) %all-gather.6.cloned.1.call-update) | async-done | bytes 3276816 | tf_op jit(solution)/shard_map/while/body/eval_jaxpr/all_gather | solution.py:58
  451.7 5.7 fusion.27
  457.4 1.8 constant_dynamic-slice_fusion.2
  459.2 0.0 all-gather.6.cloned.1.call-update
  459.3 61.8 %all-gather.6.cloned.1.call-done = bf16[1,1280,1280]{2,1,0:T(8,128)(2,1)} async-done(((bf16[1,160,1280]{2,1,0:T(8,128)(2,1)}), bf16[1,1280,1280]{2,1,0:T(8,128)(2,1)}) %all-gather.6.cloned.1.call-update) | async-done | bytes 3276816 | tf_op jit(solution)/shard_map/while/body/eval_jaxpr/all_gather | solution.py:58
  521.0 5.7 fusion.27
  526.7 1.8 constant_dynamic-slice_fusion.2
  528.5 0.0 all-gather.6.cloned.1.call-update
  528.6 61.8 %all-gather.6.cloned.1.call-done = bf16[1,1280,1280]{2,1,0:T(8,128)(2,1)} async-done(((bf16[1,160,1280]{2,1,0:T(8,128)(2,1)}), bf16[1,1280,1280]{2,1,0:T(8,128)(2,1)}) %all-gather.6.cloned.1.call-update) | async-done | bytes 3276816 | tf_op jit(solution)/shard_map/while/body/eval_jaxpr/all_gather | solution.py:58
  590.3 5.7 fusion.27
  596.1 1.8 constant_dynamic-slice_fusion.2
  597.8 0.0 all-gather.6.cloned.1.call-update
  597.9 61.7 %all-gather.6.cloned.1.call-done = bf16[1,1280,1280]{2,1,0:T(8,128)(2,1)} async-done(((bf16[1,160,1280]{2,1,0:T(8,128)(2,1)}), bf16[1,1280,1280]{2,1,0:T(8,128)(2,1)}) %all-gather.6.cloned.1.call-update) | async-done | bytes 3276816 | tf_op jit(solution)/shard_map/while/body/eval_jaxpr/all_gather | solution.py:58
  659.7 5.7 fusion.27
  665.4 2.9 fusion.20
  (19 shorter events, 0.0 us)
Async XLA Ops:
  6.5 12.2 %copy-start = (bf16[6,2,32,1280]{3,2,1,0:T(8,128)(2,1)S(1)}, bf16[6,2,32,1280]{3,2,1,0:T(8,128)(2,1)}, u32[]{:S(2)}) copy-start(bf16[6,2,32,1280]{3,2,1,0:T(8,128)(2,1)} %param.8) | copy-start | bytes 2949124
  6.5 19.0 %copy-start.2 = (f32[1280]{0:T(1024)S(1)}, f32[1280]{0:T(1024)}, u32[]{:S(2)}) copy-start(f32[1280]{0:T(1024)} %param.11) | copy-start | bytes 15364
  6.5 19.0 %copy-start.3 = (f32[1280]{0:T(1024)S(1)}, f32[1280]{0:T(1024)}, u32[]{:S(2)}) copy-start(f32[1280]{0:T(1024)} %param.10) | copy-start | bytes 15364
  27.2 3.3 collective-permute-start
  28.9 3.9 collective-permute-start.1
  34.7 630.7 %copy-start.1 = (f32[6,1280]{1,0:T(8,128)S(1)}, f32[6,1280]{1,0:T(8,128)}, u32[]{:S(2)}) copy-start(f32[6,1280]{1,0:T(8,128)} %param.13) | copy-start | bytes 92164
  34.7 71.9 %all-gather.6.cloned.1.call-start = ((), (), s32[]{:S(2)}) async-start(), calls=%async_computation | async-start | bytes 3686400 | tf_op jit(solution)/shard_map/while/body/eval_jaxpr/all_gather | solution.py:58
  111.8 63.6 %all-gather.6.cloned.1.call-start = ((), (), s32[]{:S(2)}) async-start(), calls=%async_computation | async-start | bytes 3686400 | tf_op jit(solution)/shard_map/while/body/eval_jaxpr/all_gather | solution.py:58
  181.1 63.6 %all-gather.6.cloned.1.call-start = ((), (), s32[]{:S(2)}) async-start(), calls=%async_computation | async-start | bytes 3686400 | tf_op jit(solution)/shard_map/while/body/eval_jaxpr/all_gather | solution.py:58
  250.4 63.3 %all-gather.6.cloned.1.call-start = ((), (), s32[]{:S(2)}) async-start(), calls=%async_computation | async-start | bytes 3686400 | tf_op jit(solution)/shard_map/while/body/eval_jaxpr/all_gather | solution.py:58
  319.4 63.3 %all-gather.6.cloned.1.call-start = ((), (), s32[]{:S(2)}) async-start(), calls=%async_computation | async-start | bytes 3686400 | tf_op jit(solution)/shard_map/while/body/eval_jaxpr/all_gather | solution.py:58
  388.4 63.3 %all-gather.6.cloned.1.call-start = ((), (), s32[]{:S(2)}) async-start(), calls=%async_computation | async-start | bytes 3686400 | tf_op jit(solution)/shard_map/while/body/eval_jaxpr/all_gather | solution.py:58
  457.4 63.6 %all-gather.6.cloned.1.call-start = ((), (), s32[]{:S(2)}) async-start(), calls=%async_computation | async-start | bytes 3686400 | tf_op jit(solution)/shard_map/while/body/eval_jaxpr/all_gather | solution.py:58
  526.7 63.6 %all-gather.6.cloned.1.call-start = ((), (), s32[]{:S(2)}) async-start(), calls=%async_computation | async-start | bytes 3686400 | tf_op jit(solution)/shard_map/while/body/eval_jaxpr/all_gather | solution.py:58
  596.1 63.6 %all-gather.6.cloned.1.call-start = ((), (), s32[]{:S(2)}) async-start(), calls=%async_computation | async-start | bytes 3686400 | tf_op jit(solution)/shard_map/while/body/eval_jaxpr/all_gather | solution.py:58
Sparse Core Ops, SparseCore 0:
  37.7 68.8 all-gather.5
  114.8 60.5 all-gather.5
  184.1 60.5 all-gather.5
  253.1 60.5 all-gather.5
  322.1 60.5 all-gather.5
  391.1 60.5 all-gather.5
  460.4 60.5 all-gather.5
  529.8 60.5 all-gather.5
  599.1 60.5 all-gather.5
where the time goes:
time: 675 us
  waiting for transfers between devices  566 us (84%)
  matrix products  50.9 us (8%)
  local copies, waits for them, and re-layouts  18.2 us (3%)
  blocking collectives  14.1 us (2%)
  between operations  13.2 us (2%)
  other arithmetic  9.07 us (1%)
    all_gather x9, waiting for transfers between devices, add_tap(): lax.all_gather(panel, 'dp', axis=0, tiled=True)  563 us
    dot_general x9, matrix products, tap_product(): lax.dot_general(window, panel, (((3,), (1,)), ((), ())), preferred_elemen...  50.9 us
    dynamic_slice x9, local copies, waits for them, and re-layouts, add_tap(): panel = lax.dynamic_index_in_dim(conv_weight, index, 0, keepdims=False)  16 us
  transfers between devices with their start and end apart: 11, of which 11 were waited for; matrix products, arithmetic and copies ran while one was open for 0% of the time, Pallas kernels for 0%

commit v1 on v0

--- a/solution.py
+++ b/solution.py
@@ -55,7 +55,39 @@
             padded, (0, index // 3, index % 3, 0), (frames, rows, cols, chans)
         )
         panel = lax.dynamic_index_in_dim(conv_weight, index, 0, keepdims=False)
-        return accum + tap_product(window, lax.all_gather(panel, "dp", axis=0, tiled=True))
+
+        def load_slabs(block_in, along_dim):
+            carry, near, k_now = (
+                lax.psum(1, "dp"),
+                lax.axis_index("dp"),
+                block_in.shape[along_dim],
+            )
+            pages = [
+                m * carry if dev_j == along_dim else m for dev_j, m in enumerate(block_in.shape)
+            ]
+            local_next = lax.dynamic_update_slice_in_dim(
+                jnp.zeros(pages, block_in.dtype), block_in, near * k_now, axis=along_dim
+            )
+            val = s_next = block_in
+            for kk in range(1, carry // 2 + 1):
+                val = lax.ppermute(
+                    val, "dp", [(dev_j, (dev_j + 1) % carry) for dev_j in range(carry)]
+                )
+                local_next = lax.dynamic_update_slice_in_dim(
+                    local_next, val, (near - kk) % carry * k_now, axis=along_dim
+                )
+                if 2 * kk < carry:
+                    s_next = lax.ppermute(
+                        s_next,
+                        axis_name="dp",
+                        perm=[(dev_j, (dev_j - 1) % carry) for dev_j in range(carry)],
+                    )
+                    local_next = lax.dynamic_update_slice_in_dim(
+                        local_next, s_next, (near + kk) % carry * k_now, axis=along_dim
+                    )
+            return local_next
+
+        return accum + tap_product(window, load_slabs(panel, 0))
 
     conv = lax.fori_loop(0, 9, add_tap, jnp.zeros((frames, rows, cols, chans), jnp.float32))
     conv_out = conv.astype(jnp.bfloat16)

time: 675 us -> 703 us (1.041)
  starting transfers between devices: 3 us -> 200 us
  waiting for transfers between devices: 566 us -> 394 us
  local copies, waits for them, and re-layouts: 18.2 us -> 52.5 us
  matrix products: 50.9 us -> 29.8 us
  between operations: 13.2 us -> 0.14 us
    all_gather x9 -> x0, waiting for transfers between devices: 563 us -> none  [add_tap(): lax.all_gather(panel, 'dp', axis=0, tiled=True)]
    ppermute x0 -> x63, waiting for transfers between devices: none -> 392 us  [the longest x36 385 us: load_slabs(): lax.ppermute(val, 'dp', [(dev_j, (dev_j + 1) % carry) for dev_j in range(...]
    ppermute x0 -> x63, starting transfers between devices: none -> 197 us  [the longest x27 129 us: load_slabs(): lax.ppermute(s_next, axis_name='dp', perm=[(dev_j, (dev_j - 1) % carry) f...]
    dynamic_update_slice x0 -> x72, local copies, waits for them, and re-layouts: none -> 37.6 us  [the longest x9 16.3 us: load_slabs(): lax.dynamic_update_slice_in_dim(jnp.zeros(pages, block_in.dtype), block_i...]
    dot_general x9, matrix products: 50.9 us -> 29.8 us  [tap_product(): lax.dot_general(window, panel, (((3,), (1,)), ((), ())), preferred_elemen...]
    dynamic_slice x9 -> x0, local copies, waits for them, and re-layouts: 16 us -> none  [add_tap(): panel = lax.dynamic_index_in_dim(conv_weight, index, 0, keepdims=False)]
    while x0 -> x36, local copies, waits for them, and re-layouts: none -> 11.5 us
  transfers between devices with their start and end apart: 11 -> 65, of which waited for: 11 -> 46; matrix products, arithmetic and copies ran while one was open for 0% -> 3% of each run, Pallas kernels for 0% -> 0%
where the time goes in v1:
time: 703 us; the launch traced here: 702 us
  waiting for transfers between devices  394 us (56%)
  starting transfers between devices  200 us (28%)
  local copies, waits for them, and re-layouts  52.5 us (7%)
  matrix products  29.8 us (4%)
  blocking collectives  14.2 us (2%)
  other arithmetic  10.5 us (1%)
    ppermute x36, waiting for transfers between devices, load_slabs(): lax.ppermute(val, 'dp', [(dev_j, (dev_j + 1) % carry) for dev_j in range(...  385 us
    ppermute x27, starting transfers between devices, load_slabs(): lax.ppermute(s_next, axis_name='dp', perm=[(dev_j, (dev_j - 1) % carry) f...  129 us
    ppermute x36, starting transfers between devices, load_slabs(): lax.ppermute(val, 'dp', [(dev_j, (dev_j + 1) % carry) for dev_j in range(...  67.7 us
    dot_general x9, matrix products, tap_product(): lax.dot_general(window, panel, (((3,), (1,)), ((), ())), preferred_elemen...  29.8 us
    dynamic_update_slice x9, local copies, waits for them, and re-layouts, load_slabs(): lax.dynamic_update_slice_in_dim(jnp.zeros(pages, block_in.dtype), block_i...  16.3 us
  transfers between devices with their start and end apart: 65, of which 46 were waited for; matrix products, arithmetic and copies ran while one was open for 3% of the time, Pallas kernels for 0%

profile of v1, /device:TPU:0, one launch (start us, length us, event | category | flops | bytes accessed | tf_op | source)
XLA Modules:
  0.0 701.5 jit_solution(13000951304614980459)
XLA Ops:
  3.6 8.4 %psum.14 = f32[6,32]{1,0:T(8,128)S(1)} all-reduce(f32[6,32]{1,0:T(8,128)S(1)} %reduce_sum.25), channel_id=1, replica_groups=mesh['dp'=8,'space'=4] {'space'}, use_global_device_ids=true, to_apply=%region_2.0 | all-reduce | flops 192 | bytes 1536 | tf_op jit(solution)/shard_map/psum | solution.py:41
  14.1 5.8 psum.15
  28.6 669.7 %while.17 = (s32[]{:T(128)}, f32[6,2,32,1280]{3,2,1,0:T(8,128)}, bf16[6,4,34,1280]{3,2,1,0:T(8,128)(2,1)}, bf16[9,160,1280]{2,1,0:T(8,128)(2,1)}, s32[]{:T(128)}...) while((s32[]{:T(128)}, f32[6,2,32,1280]{3,2,1,0:T(8,128)}, ...), condition=%wide.region_7.8_spmd.clone, body=%wide.region_6.7_spmd.clone.sunk | while | flops 1259274368 | bytes 45631428 | solution.py:92
  35.3 13.2 %collective-permute-done = bf16[160,1280]{1,0:T(8,128)(2,1)} collective-permute-done((bf16[160,1280]{1,0:T(8,128)(2,1)}, bf16[160,1280]{1,0:T(8,128)(2,1)}, u32[]{:S(2)}, u32[]{:S(2)}) %collective-permute-start) | collective-permute-done | bytes 409632 | tf_op jit(solution)/shard_map/while/body/eval_jaxpr/ppermute | solution.py:73
  56.2 12.3 %collective-permute-done.2 = bf16[160,1280]{1,0:T(8,128)(2,1)S(1)} collective-permute-done((bf16[160,1280]{1,0:T(8,128)(2,1)}, bf16[160,1280]{1,0:T(8,128)(2,1)S(1)}, u32[]{:S(2)}, u32[]{:S(2)}) %collective-permute-start.2) | collective-permute-done | bytes 409632 | tf_op jit(solution)/shard_map/while/body/eval_jaxpr/ppermute | solution.py:73
  73.3 15.9 %collective-permute-done.4 = bf16[160,1280]{1,0:T(8,128)(2,1)S(1)} collective-permute-done((bf16[160,1280]{1,0:T(8,128)(2,1)S(1)}, bf16[160,1280]{1,0:T(8,128)(2,1)S(1)}, u32[]{:S(2)}, u32[]{:S(2)}) %collective-permute-start.4) | collective-permute-done | bytes 409632 | tf_op jit(solution)/shard_map/while/body/eval_jaxpr/ppermute | solution.py:73
  92.3 11.4 %collective-permute-done.6 = bf16[160,1280]{1,0:T(8,128)(2,1)S(1)} collective-permute-done((bf16[160,1280]{1,0:T(8,128)(2,1)S(1)}, bf16[160,1280]{1,0:T(8,128)(2,1)S(1)}, u32[]{:S(2)}, u32[]{:S(2)}) %collective-permute-start.6) | collective-permute-done | bytes 409632 | tf_op jit(solution)/shard_map/while/body/eval_jaxpr/ppermute | solution.py:73
  103.8 3.3 fusion.27
  110.4 4.7 collective-permute-start.1
  115.2 13.3 %collective-permute-done = bf16[160,1280]{1,0:T(8,128)(2,1)} collective-permute-done((bf16[160,1280]{1,0:T(8,128)(2,1)}, bf16[160,1280]{1,0:T(8,128)(2,1)}, u32[]{:S(2)}, u32[]{:S(2)}) %collective-permute-start) | collective-permute-done | bytes 409632 | tf_op jit(solution)/shard_map/while/body/eval_jaxpr/ppermute | solution.py:73
  135.4 12.7 %collective-permute-done.2 = bf16[160,1280]{1,0:T(8,128)(2,1)S(1)} collective-permute-done((bf16[160,1280]{1,0:T(8,128)(2,1)}, bf16[160,1280]{1,0:T(8,128)(2,1)S(1)}, u32[]{:S(2)}, u32[]{:S(2)}) %collective-permute-start.2) | collective-permute-done | bytes 409632 | tf_op jit(solution)/shard_map/while/body/eval_jaxpr/ppermute | solution.py:73
  152.9 14.3 %collective-permute-done.4 = bf16[160,1280]{1,0:T(8,128)(2,1)S(1)} collective-permute-done((bf16[160,1280]{1,0:T(8,128)(2,1)S(1)}, bf16[160,1280]{1,0:T(8,128)(2,1)S(1)}, u32[]{:S(2)}, u32[]{:S(2)}) %collective-permute-start.4) | collective-permute-done | bytes 409632 | tf_op jit(solution)/shard_map/while/body/eval_jaxpr/ppermute | solution.py:73
  169.9 10.5 %collective-permute-done.6 = bf16[160,1280]{1,0:T(8,128)(2,1)S(1)} collective-permute-done((bf16[160,1280]{1,0:T(8,128)(2,1)S(1)}, bf16[160,1280]{1,0:T(8,128)(2,1)S(1)}, u32[]{:S(2)}, u32[]{:S(2)}) %collective-permute-start.6) | collective-permute-done | bytes 409632 | tf_op jit(solution)/shard_map/while/body/eval_jaxpr/ppermute | solution.py:73
  180.4 3.3 fusion.27
  187.0 4.7 collective-permute-start.1
  191.7 11.7 %collective-permute-done = bf16[160,1280]{1,0:T(8,128)(2,1)} collective-permute-done((bf16[160,1280]{1,0:T(8,128)(2,1)}, bf16[160,1280]{1,0:T(8,128)(2,1)}, u32[]{:S(2)}, u32[]{:S(2)}) %collective-permute-start) | collective-permute-done | bytes 409632 | tf_op jit(solution)/shard_map/while/body/eval_jaxpr/ppermute | solution.py:73
  205.8 7.5 %collective-permute-start.3 = (bf16[160,1280]{1,0:T(8,128)(2,1)}, bf16[160,1280]{1,0:T(8,128)(2,1)S(1)}, u32[]{:S(2)}, u32[]{:S(2)}) collective-permute-start(bf16[160,1280]{1,0:T(8,128)(2,1)} %collective-permute-done.1), channel_id=1, source_target_pairs={{0,28},{4,0},{8,4},{12,8},{16,12},{20,16},{24,20},{28,24},{1,29},{... | collective-permute-start | bytes 1228808 | tf_op jit(solution)/shard_map/while/body/eval_jaxpr/ppermute | solution.py:80
  215.6 6.6 collective-permute-done.2
  224.6 9.2 %collective-permute-start.5 = (bf16[160,1280]{1,0:T(8,128)(2,1)S(1)}, bf16[160,1280]{1,0:T(8,128)(2,1)S(1)}, u32[]{:S(2)}, u32[]{:S(2)}) collective-permute-start(bf16[160,1280]{1,0:T(8,128)(2,1)S(1)} %collective-permute-done.3), channel_id=1, source_target_pairs={{0,28},{4,0},{8,4},{12,8},{16,12},{20,16},{24,20},{28,24},{1,29},{... | collective-permute-start | bytes 1228808 | tf_op jit(solution)/shard_map/while/body/eval_jaxpr/ppermute | solution.py:80
  233.9 7.4 %collective-permute-done.4 = bf16[160,1280]{1,0:T(8,128)(2,1)S(1)} collective-permute-done((bf16[160,1280]{1,0:T(8,128)(2,1)S(1)}, bf16[160,1280]{1,0:T(8,128)(2,1)S(1)}, u32[]{:S(2)}, u32[]{:S(2)}) %collective-permute-start.4) | collective-permute-done | bytes 409632 | tf_op jit(solution)/shard_map/while/body/eval_jaxpr/ppermute | solution.py:73
  243.9 10.5 %collective-permute-done.6 = bf16[160,1280]{1,0:T(8,128)(2,1)S(1)} collective-permute-done((bf16[160,1280]{1,0:T(8,128)(2,1)S(1)}, bf16[160,1280]{1,0:T(8,128)(2,1)S(1)}, u32[]{:S(2)}, u32[]{:S(2)}) %collective-permute-start.6) | collective-permute-done | bytes 409632 | tf_op jit(solution)/shard_map/while/body/eval_jaxpr/ppermute | solution.py:73
  254.4 3.3 fusion.27
  261.1 4.7 collective-permute-start.1
  265.8 11.7 %collective-permute-done = bf16[160,1280]{1,0:T(8,128)(2,1)} collective-permute-done((bf16[160,1280]{1,0:T(8,128)(2,1)}, bf16[160,1280]{1,0:T(8,128)(2,1)}, u32[]{:S(2)}, u32[]{:S(2)}) %collective-permute-start) | collective-permute-done | bytes 409632 | tf_op jit(solution)/shard_map/while/body/eval_jaxpr/ppermute | solution.py:73
  285.2 11.0 %collective-permute-done.2 = bf16[160,1280]{1,0:T(8,128)(2,1)S(1)} collective-permute-done((bf16[160,1280]{1,0:T(8,128)(2,1)}, bf16[160,1280]{1,0:T(8,128)(2,1)S(1)}, u32[]{:S(2)}, u32[]{:S(2)}) %collective-permute-start.2) | collective-permute-done | bytes 409632 | tf_op jit(solution)/shard_map/while/body/eval_jaxpr/ppermute | solution.py:73
  298.6 3.9 collective-permute-start.5
  302.6 12.7 %collective-permute-done.4 = bf16[160,1280]{1,0:T(8,128)(2,1)S(1)} collective-permute-done((bf16[160,1280]{1,0:T(8,128)(2,1)S(1)}, bf16[160,1280]{1,0:T(8,128)(2,1)S(1)}, u32[]{:S(2)}, u32[]{:S(2)}) %collective-permute-start.4) | collective-permute-done | bytes 409632 | tf_op jit(solution)/shard_map/while/body/eval_jaxpr/ppermute | solution.py:73
  317.9 10.5 %collective-permute-done.6 = bf16[160,1280]{1,0:T(8,128)(2,1)S(1)} collective-permute-done((bf16[160,1280]{1,0:T(8,128)(2,1)S(1)}, bf16[160,1280]{1,0:T(8,128)(2,1)S(1)}, u32[]{:S(2)}, u32[]{:S(2)}) %collective-permute-start.6) | collective-permute-done | bytes 409632 | tf_op jit(solution)/shard_map/while/body/eval_jaxpr/ppermute | solution.py:73
  328.5 3.3 fusion.27
  335.1 4.7 collective-permute-start.1
  339.9 11.2 %collective-permute-done = bf16[160,1280]{1,0:T(8,128)(2,1)} collective-permute-done((bf16[160,1280]{1,0:T(8,128)(2,1)}, bf16[160,1280]{1,0:T(8,128)(2,1)}, u32[]{:S(2)}, u32[]{:S(2)}) %collective-permute-start) | collective-permute-done | bytes 409632 | tf_op jit(solution)/shard_map/while/body/eval_jaxpr/ppermute | solution.py:73
  358.7 10.6 %collective-permute-done.2 = bf16[160,1280]{1,0:T(8,128)(2,1)S(1)} collective-permute-done((bf16[160,1280]{1,0:T(8,128)(2,1)}, bf16[160,1280]{1,0:T(8,128)(2,1)S(1)}, u32[]{:S(2)}, u32[]{:S(2)}) %collective-permute-start.2) | collective-permute-done | bytes 409632 | tf_op jit(solution)/shard_map/while/body/eval_jaxpr/ppermute | solution.py:73
  374.9 13.5 %collective-permute-done.4 = bf16[160,1280]{1,0:T(8,128)(2,1)S(1)} collective-permute-done((bf16[160,1280]{1,0:T(8,128)(2,1)S(1)}, bf16[160,1280]{1,0:T(8,128)(2,1)S(1)}, u32[]{:S(2)}, u32[]{:S(2)}) %collective-permute-start.4) | collective-permute-done | bytes 409632 | tf_op jit(solution)/shard_map/while/body/eval_jaxpr/ppermute | solution.py:73
  391.1 10.4 %collective-permute-done.6 = bf16[160,1280]{1,0:T(8,128)(2,1)S(1)} collective-permute-done((bf16[160,1280]{1,0:T(8,128)(2,1)S(1)}, bf16[160,1280]{1,0:T(8,128)(2,1)S(1)}, u32[]{:S(2)}, u32[]{:S(2)}) %collective-permute-start.6) | collective-permute-done | bytes 409632 | tf_op jit(solution)/shard_map/while/body/eval_jaxpr/ppermute | solution.py:73
  401.5 3.3 fusion.27
  408.1 4.7 collective-permute-start.1
  412.9 11.6 %collective-permute-done = bf16[160,1280]{1,0:T(8,128)(2,1)} collective-permute-done((bf16[160,1280]{1,0:T(8,128)(2,1)}, bf16[160,1280]{1,0:T(8,128)(2,1)}, u32[]{:S(2)}, u32[]{:S(2)}) %collective-permute-start) | collective-permute-done | bytes 409632 | tf_op jit(solution)/shard_map/while/body/eval_jaxpr/ppermute | solution.py:73
  431.4 12.1 %collective-permute-done.2 = bf16[160,1280]{1,0:T(8,128)(2,1)S(1)} collective-permute-done((bf16[160,1280]{1,0:T(8,128)(2,1)}, bf16[160,1280]{1,0:T(8,128)(2,1)S(1)}, u32[]{:S(2)}, u32[]{:S(2)}) %collective-permute-start.2) | collective-permute-done | bytes 409632 | tf_op jit(solution)/shard_map/while/body/eval_jaxpr/ppermute | solution.py:73
  448.3 13.8 %collective-permute-done.4 = bf16[160,1280]{1,0:T(8,128)(2,1)S(1)} collective-permute-done((bf16[160,1280]{1,0:T(8,128)(2,1)S(1)}, bf16[160,1280]{1,0:T(8,128)(2,1)S(1)}, u32[]{:S(2)}, u32[]{:S(2)}) %collective-permute-start.4) | collective-permute-done | bytes 409632 | tf_op jit(solution)/shard_map/while/body/eval_jaxpr/ppermute | solution.py:73
  464.8 10.0 %collective-permute-done.6 = bf16[160,1280]{1,0:T(8,128)(2,1)S(1)} collective-permute-done((bf16[160,1280]{1,0:T(8,128)(2,1)S(1)}, bf16[160,1280]{1,0:T(8,128)(2,1)S(1)}, u32[]{:S(2)}, u32[]{:S(2)}) %collective-permute-start.6) | collective-permute-done | bytes 409632 | tf_op jit(solution)/shard_map/while/body/eval_jaxpr/ppermute | solution.py:73
  481.5 4.7 collective-permute-start.1
  486.2 11.4 %collective-permute-done = bf16[160,1280]{1,0:T(8,128)(2,1)} collective-permute-done((bf16[160,1280]{1,0:T(8,128)(2,1)}, bf16[160,1280]{1,0:T(8,128)(2,1)}, u32[]{:S(2)}, u32[]{:S(2)}) %collective-permute-start) | collective-permute-done | bytes 409632 | tf_op jit(solution)/shard_map/while/body/eval_jaxpr/ppermute | solution.py:73
  500.1 10.2 %collective-permute-start.3 = (bf16[160,1280]{1,0:T(8,128)(2,1)}, bf16[160,1280]{1,0:T(8,128)(2,1)S(1)}, u32[]{:S(2)}, u32[]{:S(2)}) collective-permute-start(bf16[160,1280]{1,0:T(8,128)(2,1)} %collective-permute-done.1), channel_id=1, source_target_pairs={{0,28},{4,0},{8,4},{12,8},{16,12},{20,16},{24,20},{28,24},{1,29},{... | collective-permute-start | bytes 1228808 | tf_op jit(solution)/shard_map/while/body/eval_jaxpr/ppermute | solution.py:80
  512.5 3.9 collective-permute-done.2
  518.8 11.9 %collective-permute-start.5 = (bf16[160,1280]{1,0:T(8,128)(2,1)S(1)}, bf16[160,1280]{1,0:T(8,128)(2,1)S(1)}, u32[]{:S(2)}, u32[]{:S(2)}) collective-permute-start(bf16[160,1280]{1,0:T(8,128)(2,1)S(1)} %collective-permute-done.3), channel_id=1, source_target_pairs={{0,28},{4,0},{8,4},{12,8},{16,12},{20,16},{24,20},{28,24},{1,29},{... | collective-permute-start | bytes 1228808 | tf_op jit(solution)/shard_map/while/body/eval_jaxpr/ppermute | solution.py:80
  530.8 3.8 collective-permute-done.4
  538.8 8.3 %collective-permute-done.6 = bf16[160,1280]{1,0:T(8,128)(2,1)S(1)} collective-permute-done((bf16[160,1280]{1,0:T(8,128)(2,1)S(1)}, bf16[160,1280]{1,0:T(8,128)(2,1)S(1)}, u32[]{:S(2)}, u32[]{:S(2)}) %collective-permute-start.6) | collective-permute-done | bytes 409632 | tf_op jit(solution)/shard_map/while/body/eval_jaxpr/ppermute | solution.py:73
  547.2 3.3 fusion.27
  553.8 5.1 collective-permute-start.1
  559.0 10.6 %collective-permute-done = bf16[160,1280]{1,0:T(8,128)(2,1)} collective-permute-done((bf16[160,1280]{1,0:T(8,128)(2,1)}, bf16[160,1280]{1,0:T(8,128)(2,1)}, u32[]{:S(2)}, u32[]{:S(2)}) %collective-permute-start) | collective-permute-done | bytes 409632 | tf_op jit(solution)/shard_map/while/body/eval_jaxpr/ppermute | solution.py:73
  572.1 6.9 collective-permute-start.3
  581.1 7.3 %collective-permute-done.2 = bf16[160,1280]{1,0:T(8,128)(2,1)S(1)} collective-permute-done((bf16[160,1280]{1,0:T(8,128)(2,1)}, bf16[160,1280]{1,0:T(8,128)(2,1)S(1)}, u32[]{:S(2)}, u32[]{:S(2)}) %collective-permute-start.2) | collective-permute-done | bytes 409632 | tf_op jit(solution)/shard_map/while/body/eval_jaxpr/ppermute | solution.py:73
  590.8 7.0 %collective-permute-start.5 = (bf16[160,1280]{1,0:T(8,128)(2,1)S(1)}, bf16[160,1280]{1,0:T(8,128)(2,1)S(1)}, u32[]{:S(2)}, u32[]{:S(2)}) collective-permute-start(bf16[160,1280]{1,0:T(8,128)(2,1)S(1)} %collective-permute-done.3), channel_id=1, source_target_pairs={{0,28},{4,0},{8,4},{12,8},{16,12},{20,16},{24,20},{28,24},{1,29},{... | collective-permute-start | bytes 1228808 | tf_op jit(solution)/shard_map/while/body/eval_jaxpr/ppermute | solution.py:80
  597.9 8.7 %collective-permute-done.4 = bf16[160,1280]{1,0:T(8,128)(2,1)S(1)} collective-permute-done((bf16[160,1280]{1,0:T(8,128)(2,1)S(1)}, bf16[160,1280]{1,0:T(8,128)(2,1)S(1)}, u32[]{:S(2)}, u32[]{:S(2)}) %collective-permute-start.4) | collective-permute-done | bytes 409632 | tf_op jit(solution)/shard_map/while/body/eval_jaxpr/ppermute | solution.py:73
  609.2 12.9 %collective-permute-done.6 = bf16[160,1280]{1,0:T(8,128)(2,1)S(1)} collective-permute-done((bf16[160,1280]{1,0:T(8,128)(2,1)S(1)}, bf16[160,1280]{1,0:T(8,128)(2,1)S(1)}, u32[]{:S(2)}, u32[]{:S(2)}) %collective-permute-start.6) | collective-permute-done | bytes 409632 | tf_op jit(solution)/shard_map/while/body/eval_jaxpr/ppermute | solution.py:73
  622.1 3.3 fusion.27
  628.8 4.7 collective-permute-start.1
  633.5 8.9 %collective-permute-done = bf16[160,1280]{1,0:T(8,128)(2,1)} collective-permute-done((bf16[160,1280]{1,0:T(8,128)(2,1)}, bf16[160,1280]{1,0:T(8,128)(2,1)}, u32[]{:S(2)}, u32[]{:S(2)}) %collective-permute-start) | collective-permute-done | bytes 409632 | tf_op jit(solution)/shard_map/while/body/eval_jaxpr/ppermute | solution.py:73
  644.9 5.5 collective-permute-start.3
  652.6 9.0 %collective-permute-done.2 = bf16[160,1280]{1,0:T(8,128)(2,1)S(1)} collective-permute-done((bf16[160,1280]{1,0:T(8,128)(2,1)}, bf16[160,1280]{1,0:T(8,128)(2,1)S(1)}, u32[]{:S(2)}, u32[]{:S(2)}) %collective-permute-start.2) | collective-permute-done | bytes 409632 | tf_op jit(solution)/shard_map/while/body/eval_jaxpr/ppermute | solution.py:73
  664.0 5.4 collective-permute-start.5
  669.5 11.1 %collective-permute-done.4 = bf16[160,1280]{1,0:T(8,128)(2,1)S(1)} collective-permute-done((bf16[160,1280]{1,0:T(8,128)(2,1)S(1)}, bf16[160,1280]{1,0:T(8,128)(2,1)S(1)}, u32[]{:S(2)}, u32[]{:S(2)}) %collective-permute-start.4) | collective-permute-done | bytes 409632 | tf_op jit(solution)/shard_map/while/body/eval_jaxpr/ppermute | solution.py:73
  683.1 10.5 %collective-permute-done.6 = bf16[160,1280]{1,0:T(8,128)(2,1)S(1)} collective-permute-done((bf16[160,1280]{1,0:T(8,128)(2,1)S(1)}, bf16[160,1280]{1,0:T(8,128)(2,1)S(1)}, u32[]{:S(2)}, u32[]{:S(2)}) %collective-permute-start.6) | collective-permute-done | bytes 409632 | tf_op jit(solution)/shard_map/while/body/eval_jaxpr/ppermute | solution.py:73
  693.7 3.3 fusion.27
  (226 shorter events, 169.2 us)
Async XLA Ops:
  22.8 3.9 collective-permute-start.8
  30.6 17.9 %collective-permute-start = (bf16[160,1280]{1,0:T(8,128)(2,1)}, bf16[160,1280]{1,0:T(8,128)(2,1)}, u32[]{:S(2)}, u32[]{:S(2)}) collective-permute-start(bf16[160,1280]{1,0:T(8,128)(2,1)} %get-tuple-element.211), channel_id=1, source_target_pairs={{0,4},{4,8},{8,12},{12,16},{16,20},{20,24},{24,28},{28,0},{1,5},{5... | collective-permute-start | bytes 1228808 | tf_op jit(solution)/shard_map/while/body/eval_jaxpr/ppermute | solution.py:73
  32.2 20.1 %collective-permute-start.1 = (bf16[160,1280]{1,0:T(8,128)(2,1)}, bf16[160,1280]{1,0:T(8,128)(2,1)}, u32[]{:S(2)}, u32[]{:S(2)}) collective-permute-start(bf16[160,1280]{1,0:T(8,128)(2,1)} %get-tuple-element.211), channel_id=1, source_target_pairs={{0,28},{4,0},{8,4},{12,8},{16,12},{20,16},{24,20},{28,24},{1,29},{... | collective-permute-start | bytes 1228808 | tf_op jit(solution)/shard_map/while/body/eval_jaxpr/ppermute | solution.py:80
  48.5 19.9 %collective-permute-start.2 = (bf16[160,1280]{1,0:T(8,128)(2,1)}, bf16[160,1280]{1,0:T(8,128)(2,1)S(1)}, u32[]{:S(2)}, u32[]{:S(2)}) collective-permute-start(bf16[160,1280]{1,0:T(8,128)(2,1)} %collective-permute-done), channel_id=1, source_target_pairs={{0,4},{4,8},{8,12},{12,16},{16,20},{20,24},{24,28},{28,0},{1,5},{5... | collective-permute-start | bytes 1228808 | tf_op jit(solution)/shard_map/while/body/eval_jaxpr/ppermute | solution.py:73
  52.3 20.7 %collective-permute-start.3 = (bf16[160,1280]{1,0:T(8,128)(2,1)}, bf16[160,1280]{1,0:T(8,128)(2,1)S(1)}, u32[]{:S(2)}, u32[]{:S(2)}) collective-permute-start(bf16[160,1280]{1,0:T(8,128)(2,1)} %collective-permute-done.1), channel_id=1, source_target_pairs={{0,28},{4,0},{8,4},{12,8},{16,12},{20,16},{24,20},{28,24},{1,29},{... | collective-permute-start | bytes 1228808 | tf_op jit(solution)/shard_map/while/body/eval_jaxpr/ppermute | solution.py:80
  68.4 20.7 %collective-permute-start.4 = (bf16[160,1280]{1,0:T(8,128)(2,1)S(1)}, bf16[160,1280]{1,0:T(8,128)(2,1)S(1)}, u32[]{:S(2)}, u32[]{:S(2)}) collective-permute-start(bf16[160,1280]{1,0:T(8,128)(2,1)S(1)} %collective-permute-done.2), channel_id=1, source_target_pairs={{0,4},{4,8},{8,12},{12,16},{16,20},{20,24},{24,28},{28,0},{1,5},{5... | collective-permute-start | bytes 1228808 | tf_op jit(solution)/shard_map/while/body/eval_jaxpr/ppermute | solution.py:73
  73.0 19.3 %collective-permute-start.5 = (bf16[160,1280]{1,0:T(8,128)(2,1)S(1)}, bf16[160,1280]{1,0:T(8,128)(2,1)S(1)}, u32[]{:S(2)}, u32[]{:S(2)}) collective-permute-start(bf16[160,1280]{1,0:T(8,128)(2,1)S(1)} %collective-permute-done.3), channel_id=1, source_target_pairs={{0,28},{4,0},{8,4},{12,8},{16,12},{20,16},{24,20},{28,24},{1,29},{... | collective-permute-start | bytes 1228808 | tf_op jit(solution)/shard_map/while/body/eval_jaxpr/ppermute | solution.py:80
  89.2 14.6 %collective-permute-start.6 = (bf16[160,1280]{1,0:T(8,128)(2,1)S(1)}, bf16[160,1280]{1,0:T(8,128)(2,1)S(1)}, u32[]{:S(2)}, u32[]{:S(2)}) collective-permute-start(bf16[160,1280]{1,0:T(8,128)(2,1)S(1)} %collective-permute-done.4), channel_id=1, source_target_pairs={{0,4},{4,8},{8,12},{12,16},{16,20},{20,24},{24,28},{28,0},{1,5},{5... | collective-permute-start | bytes 1228808 | tf_op jit(solution)/shard_map/while/body/eval_jaxpr/ppermute | solution.py:73
  110.4 18.0 %collective-permute-start = (bf16[160,1280]{1,0:T(8,128)(2,1)}, bf16[160,1280]{1,0:T(8,128)(2,1)}, u32[]{:S(2)}, u32[]{:S(2)}) collective-permute-start(bf16[160,1280]{1,0:T(8,128)(2,1)} %get-tuple-element.211), channel_id=1, source_target_pairs={{0,4},{4,8},{8,12},{12,16},{16,20},{20,24},{24,28},{28,0},{1,5},{5... | collective-permute-start | bytes 1228808 | tf_op jit(solution)/shard_map/while/body/eval_jaxpr/ppermute | solution.py:73
  110.4 20.5 %collective-permute-start.1 = (bf16[160,1280]{1,0:T(8,128)(2,1)}, bf16[160,1280]{1,0:T(8,128)(2,1)}, u32[]{:S(2)}, u32[]{:S(2)}) collective-permute-start(bf16[160,1280]{1,0:T(8,128)(2,1)} %get-tuple-element.211), channel_id=1, source_target_pairs={{0,28},{4,0},{8,4},{12,8},{16,12},{20,16},{24,20},{28,24},{1,29},{... | collective-permute-start | bytes 1228808 | tf_op jit(solution)/shard_map/while/body/eval_jaxpr/ppermute | solution.py:80
  128.5 19.7 %collective-permute-start.2 = (bf16[160,1280]{1,0:T(8,128)(2,1)}, bf16[160,1280]{1,0:T(8,128)(2,1)S(1)}, u32[]{:S(2)}, u32[]{:S(2)}) collective-permute-start(bf16[160,1280]{1,0:T(8,128)(2,1)} %collective-permute-done), channel_id=1, source_target_pairs={{0,4},{4,8},{8,12},{12,16},{16,20},{20,24},{24,28},{28,0},{1,5},{5... | collective-permute-start | bytes 1228808 | tf_op jit(solution)/shard_map/while/body/eval_jaxpr/ppermute | solution.py:73
  130.9 19.6 %collective-permute-start.3 = (bf16[160,1280]{1,0:T(8,128)(2,1)}, bf16[160,1280]{1,0:T(8,128)(2,1)S(1)}, u32[]{:S(2)}, u32[]{:S(2)}) collective-permute-start(bf16[160,1280]{1,0:T(8,128)(2,1)} %collective-permute-done.1), channel_id=1, source_target_pairs={{0,28},{4,0},{8,4},{12,8},{16,12},{20,16},{24,20},{28,24},{1,29},{... | collective-permute-start | bytes 1228808 | tf_op jit(solution)/shard_map/while/body/eval_jaxpr/ppermute | solution.py:80
  148.1 19.1 %collective-permute-start.4 = (bf16[160,1280]{1,0:T(8,128)(2,1)S(1)}, bf16[160,1280]{1,0:T(8,128)(2,1)S(1)}, u32[]{:S(2)}, u32[]{:S(2)}) collective-permute-start(bf16[160,1280]{1,0:T(8,128)(2,1)S(1)} %collective-permute-done.2), channel_id=1, source_target_pairs={{0,4},{4,8},{8,12},{12,16},{16,20},{20,24},{24,28},{28,0},{1,5},{5... | collective-permute-start | bytes 1228808 | tf_op jit(solution)/shard_map/while/body/eval_jaxpr/ppermute | solution.py:73
  150.5 19.3 %collective-permute-start.5 = (bf16[160,1280]{1,0:T(8,128)(2,1)S(1)}, bf16[160,1280]{1,0:T(8,128)(2,1)S(1)}, u32[]{:S(2)}, u32[]{:S(2)}) collective-permute-start(bf16[160,1280]{1,0:T(8,128)(2,1)S(1)} %collective-permute-done.3), channel_id=1, source_target_pairs={{0,28},{4,0},{8,4},{12,8},{16,12},{20,16},{24,20},{28,24},{1,29},{... | collective-permute-start | bytes 1228808 | tf_op jit(solution)/shard_map/while/body/eval_jaxpr/ppermute | solution.py:80
  167.2 13.1 %collective-permute-start.6 = (bf16[160,1280]{1,0:T(8,128)(2,1)S(1)}, bf16[160,1280]{1,0:T(8,128)(2,1)S(1)}, u32[]{:S(2)}, u32[]{:S(2)}) collective-permute-start(bf16[160,1280]{1,0:T(8,128)(2,1)S(1)} %collective-permute-done.4), channel_id=1, source_target_pairs={{0,4},{4,8},{8,12},{12,16},{16,20},{20,24},{24,28},{28,0},{1,5},{5... | collective-permute-start | bytes 1228808 | tf_op jit(solution)/shard_map/while/body/eval_jaxpr/ppermute | solution.py:73
  187.0 16.4 %collective-permute-start = (bf16[160,1280]{1,0:T(8,128)(2,1)}, bf16[160,1280]{1,0:T(8,128)(2,1)}, u32[]{:S(2)}, u32[]{:S(2)}) collective-permute-start(bf16[160,1280]{1,0:T(8,128)(2,1)} %get-tuple-element.211), channel_id=1, source_target_pairs={{0,4},{4,8},{8,12},{12,16},{16,20},{20,24},{24,28},{28,0},{1,5},{5... | collective-permute-start | bytes 1228808 | tf_op jit(solution)/shard_map/while/body/eval_jaxpr/ppermute | solution.py:73
  187.0 18.9 %collective-permute-start.1 = (bf16[160,1280]{1,0:T(8,128)(2,1)}, bf16[160,1280]{1,0:T(8,128)(2,1)}, u32[]{:S(2)}, u32[]{:S(2)}) collective-permute-start(bf16[160,1280]{1,0:T(8,128)(2,1)} %get-tuple-element.211), channel_id=1, source_target_pairs={{0,28},{4,0},{8,4},{12,8},{16,12},{20,16},{24,20},{28,24},{1,29},{... | collective-permute-start | bytes 1228808 | tf_op jit(solution)/shard_map/while/body/eval_jaxpr/ppermute | solution.py:80
  203.4 18.8 %collective-permute-start.2 = (bf16[160,1280]{1,0:T(8,128)(2,1)}, bf16[160,1280]{1,0:T(8,128)(2,1)S(1)}, u32[]{:S(2)}, u32[]{:S(2)}) collective-permute-start(bf16[160,1280]{1,0:T(8,128)(2,1)} %collective-permute-done), channel_id=1, source_target_pairs={{0,4},{4,8},{8,12},{12,16},{16,20},{20,24},{24,28},{28,0},{1,5},{5... | collective-permute-start | bytes 1228808 | tf_op jit(solution)/shard_map/while/body/eval_jaxpr/ppermute | solution.py:73
  205.8 18.7 %collective-permute-start.3 = (bf16[160,1280]{1,0:T(8,128)(2,1)}, bf16[160,1280]{1,0:T(8,128)(2,1)S(1)}, u32[]{:S(2)}, u32[]{:S(2)}) collective-permute-start(bf16[160,1280]{1,0:T(8,128)(2,1)} %collective-permute-done.1), channel_id=1, source_target_pairs={{0,28},{4,0},{8,4},{12,8},{16,12},{20,16},{24,20},{28,24},{1,29},{... | collective-permute-start | bytes 1228808 | tf_op jit(solution)/shard_map/while/body/eval_jaxpr/ppermute | solution.py:80
  222.2 19.1 %collective-permute-start.4 = (bf16[160,1280]{1,0:T(8,128)(2,1)S(1)}, bf16[160,1280]{1,0:T(8,128)(2,1)S(1)}, u32[]{:S(2)}, u32[]{:S(2)}) collective-permute-start(bf16[160,1280]{1,0:T(8,128)(2,1)S(1)} %collective-permute-done.2), channel_id=1, source_target_pairs={{0,4},{4,8},{8,12},{12,16},{16,20},{20,24},{24,28},{28,0},{1,5},{5... | collective-permute-start | bytes 1228808 | tf_op jit(solution)/shard_map/while/body/eval_jaxpr/ppermute | solution.py:73
  224.6 19.3 %collective-permute-start.5 = (bf16[160,1280]{1,0:T(8,128)(2,1)S(1)}, bf16[160,1280]{1,0:T(8,128)(2,1)S(1)}, u32[]{:S(2)}, u32[]{:S(2)}) collective-permute-start(bf16[160,1280]{1,0:T(8,128)(2,1)S(1)} %collective-permute-done.3), channel_id=1, source_target_pairs={{0,28},{4,0},{8,4},{12,8},{16,12},{20,16},{24,20},{28,24},{1,29},{... | collective-permute-start | bytes 1228808 | tf_op jit(solution)/shard_map/while/body/eval_jaxpr/ppermute | solution.py:80
  241.3 13.1 %collective-permute-start.6 = (bf16[160,1280]{1,0:T(8,128)(2,1)S(1)}, bf16[160,1280]{1,0:T(8,128)(2,1)S(1)}, u32[]{:S(2)}, u32[]{:S(2)}) collective-permute-start(bf16[160,1280]{1,0:T(8,128)(2,1)S(1)} %collective-permute-done.4), channel_id=1, source_target_pairs={{0,4},{4,8},{8,12},{12,16},{16,20},{20,24},{24,28},{28,0},{1,5},{5... | collective-permute-start | bytes 1228808 | tf_op jit(solution)/shard_map/while/body/eval_jaxpr/ppermute | solution.py:73
  261.1 16.4 %collective-permute-start = (bf16[160,1280]{1,0:T(8,128)(2,1)}, bf16[160,1280]{1,0:T(8,128)(2,1)}, u32[]{:S(2)}, u32[]{:S(2)}) collective-permute-start(bf16[160,1280]{1,0:T(8,128)(2,1)} %get-tuple-element.211), channel_id=1, source_target_pairs={{0,4},{4,8},{8,12},{12,16},{16,20},{20,24},{24,28},{28,0},{1,5},{5... | collective-permute-start | bytes 1228808 | tf_op jit(solution)/shard_map/while/body/eval_jaxpr/ppermute | solution.py:73
  261.1 18.9 %collective-permute-start.1 = (bf16[160,1280]{1,0:T(8,128)(2,1)}, bf16[160,1280]{1,0:T(8,128)(2,1)}, u32[]{:S(2)}, u32[]{:S(2)}) collective-permute-start(bf16[160,1280]{1,0:T(8,128)(2,1)} %get-tuple-element.211), channel_id=1, source_target_pairs={{0,28},{4,0},{8,4},{12,8},{16,12},{20,16},{24,20},{28,24},{1,29},{... | collective-permute-start | bytes 1228808 | tf_op jit(solution)/shard_map/while/body/eval_jaxpr/ppermute | solution.py:80
  277.4 18.8 %collective-permute-start.2 = (bf16[160,1280]{1,0:T(8,128)(2,1)}, bf16[160,1280]{1,0:T(8,128)(2,1)S(1)}, u32[]{:S(2)}, u32[]{:S(2)}) collective-permute-start(bf16[160,1280]{1,0:T(8,128)(2,1)} %collective-permute-done), channel_id=1, source_target_pairs={{0,4},{4,8},{8,12},{12,16},{16,20},{20,24},{24,28},{28,0},{1,5},{5... | collective-permute-start | bytes 1228808 | tf_op jit(solution)/shard_map/while/body/eval_jaxpr/ppermute | solution.py:73
  279.9 18.7 %collective-permute-start.3 = (bf16[160,1280]{1,0:T(8,128)(2,1)}, bf16[160,1280]{1,0:T(8,128)(2,1)S(1)}, u32[]{:S(2)}, u32[]{:S(2)}) collective-permute-start(bf16[160,1280]{1,0:T(8,128)(2,1)} %collective-permute-done.1), channel_id=1, source_target_pairs={{0,28},{4,0},{8,4},{12,8},{16,12},{20,16},{24,20},{28,24},{1,29},{... | collective-permute-start | bytes 1228808 | tf_op jit(solution)/shard_map/while/body/eval_jaxpr/ppermute | solution.py:80
  296.3 19.1 %collective-permute-start.4 = (bf16[160,1280]{1,0:T(8,128)(2,1)S(1)}, bf16[160,1280]{1,0:T(8,128)(2,1)S(1)}, u32[]{:S(2)}, u32[]{:S(2)}) collective-permute-start(bf16[160,1280]{1,0:T(8,128)(2,1)S(1)} %collective-permute-done.2), channel_id=1, source_target_pairs={{0,4},{4,8},{8,12},{12,16},{16,20},{20,24},{24,28},{28,0},{1,5},{5... | collective-permute-start | bytes 1228808 | tf_op jit(solution)/shard_map/while/body/eval_jaxpr/ppermute | solution.py:73
  298.6 19.2 %collective-permute-start.5 = (bf16[160,1280]{1,0:T(8,128)(2,1)S(1)}, bf16[160,1280]{1,0:T(8,128)(2,1)S(1)}, u32[]{:S(2)}, u32[]{:S(2)}) collective-permute-start(bf16[160,1280]{1,0:T(8,128)(2,1)S(1)} %collective-permute-done.3), channel_id=1, source_target_pairs={{0,28},{4,0},{8,4},{12,8},{16,12},{20,16},{24,20},{28,24},{1,29},{... | collective-permute-start | bytes 1228808 | tf_op jit(solution)/shard_map/while/body/eval_jaxpr/ppermute | solution.py:80
  315.3 13.1 %collective-permute-start.6 = (bf16[160,1280]{1,0:T(8,128)(2,1)S(1)}, bf16[160,1280]{1,0:T(8,128)(2,1)S(1)}, u32[]{:S(2)}, u32[]{:S(2)}) collective-permute-start(bf16[160,1280]{1,0:T(8,128)(2,1)S(1)} %collective-permute-done.4), channel_id=1, source_target_pairs={{0,4},{4,8},{8,12},{12,16},{16,20},{20,24},{24,28},{28,0},{1,5},{5... | collective-permute-start | bytes 1228808 | tf_op jit(solution)/shard_map/while/body/eval_jaxpr/ppermute | solution.py:73
  335.1 15.9 %collective-permute-start = (bf16[160,1280]{1,0:T(8,128)(2,1)}, bf16[160,1280]{1,0:T(8,128)(2,1)}, u32[]{:S(2)}, u32[]{:S(2)}) collective-permute-start(bf16[160,1280]{1,0:T(8,128)(2,1)} %get-tuple-element.211), channel_id=1, source_target_pairs={{0,4},{4,8},{8,12},{12,16},{16,20},{20,24},{24,28},{28,0},{1,5},{5... | collective-permute-start | bytes 1228808 | tf_op jit(solution)/shard_map/while/body/eval_jaxpr/ppermute | solution.py:73
  335.1 18.4 %collective-permute-start.1 = (bf16[160,1280]{1,0:T(8,128)(2,1)}, bf16[160,1280]{1,0:T(8,128)(2,1)}, u32[]{:S(2)}, u32[]{:S(2)}) collective-permute-start(bf16[160,1280]{1,0:T(8,128)(2,1)} %get-tuple-element.211), channel_id=1, source_target_pairs={{0,28},{4,0},{8,4},{12,8},{16,12},{20,16},{24,20},{28,24},{1,29},{... | collective-permute-start | bytes 1228808 | tf_op jit(solution)/shard_map/while/body/eval_jaxpr/ppermute | solution.py:80
  351.0 18.3 %collective-permute-start.2 = (bf16[160,1280]{1,0:T(8,128)(2,1)}, bf16[160,1280]{1,0:T(8,128)(2,1)S(1)}, u32[]{:S(2)}, u32[]{:S(2)}) collective-permute-start(bf16[160,1280]{1,0:T(8,128)(2,1)} %collective-permute-done), channel_id=1, source_target_pairs={{0,4},{4,8},{8,12},{12,16},{16,20},{20,24},{24,28},{28,0},{1,5},{5... | collective-permute-start | bytes 1228808 | tf_op jit(solution)/shard_map/while/body/eval_jaxpr/ppermute | solution.py:73
  353.5 18.2 %collective-permute-start.3 = (bf16[160,1280]{1,0:T(8,128)(2,1)}, bf16[160,1280]{1,0:T(8,128)(2,1)S(1)}, u32[]{:S(2)}, u32[]{:S(2)}) collective-permute-start(bf16[160,1280]{1,0:T(8,128)(2,1)} %collective-permute-done.1), channel_id=1, source_target_pairs={{0,28},{4,0},{8,4},{12,8},{16,12},{20,16},{24,20},{28,24},{1,29},{... | collective-permute-start | bytes 1228808 | tf_op jit(solution)/shard_map/while/body/eval_jaxpr/ppermute | solution.py:80
  369.3 19.1 %collective-permute-start.4 = (bf16[160,1280]{1,0:T(8,128)(2,1)S(1)}, bf16[160,1280]{1,0:T(8,128)(2,1)S(1)}, u32[]{:S(2)}, u32[]{:S(2)}) collective-permute-start(bf16[160,1280]{1,0:T(8,128)(2,1)S(1)} %collective-permute-done.2), channel_id=1, source_target_pairs={{0,4},{4,8},{8,12},{12,16},{16,20},{20,24},{24,28},{28,0},{1,5},{5... | collective-permute-start | bytes 1228808 | tf_op jit(solution)/shard_map/while/body/eval_jaxpr/ppermute | solution.py:73
  371.7 19.3 %collective-permute-start.5 = (bf16[160,1280]{1,0:T(8,128)(2,1)S(1)}, bf16[160,1280]{1,0:T(8,128)(2,1)S(1)}, u32[]{:S(2)}, u32[]{:S(2)}) collective-permute-start(bf16[160,1280]{1,0:T(8,128)(2,1)S(1)} %collective-permute-done.3), channel_id=1, source_target_pairs={{0,28},{4,0},{8,4},{12,8},{16,12},{20,16},{24,20},{28,24},{1,29},{... | collective-permute-start | bytes 1228808 | tf_op jit(solution)/shard_map/while/body/eval_jaxpr/ppermute | solution.py:80
  388.4 13.0 %collective-permute-start.6 = (bf16[160,1280]{1,0:T(8,128)(2,1)S(1)}, bf16[160,1280]{1,0:T(8,128)(2,1)S(1)}, u32[]{:S(2)}, u32[]{:S(2)}) collective-permute-start(bf16[160,1280]{1,0:T(8,128)(2,1)S(1)} %collective-permute-done.4), channel_id=1, source_target_pairs={{0,4},{4,8},{8,12},{12,16},{16,20},{20,24},{24,28},{28,0},{1,5},{5... | collective-permute-start | bytes 1228808 | tf_op jit(solution)/shard_map/while/body/eval_jaxpr/ppermute | solution.py:73
  408.1 16.3 %collective-permute-start = (bf16[160,1280]{1,0:T(8,128)(2,1)}, bf16[160,1280]{1,0:T(8,128)(2,1)}, u32[]{:S(2)}, u32[]{:S(2)}) collective-permute-start(bf16[160,1280]{1,0:T(8,128)(2,1)} %get-tuple-element.211), channel_id=1, source_target_pairs={{0,4},{4,8},{8,12},{12,16},{16,20},{20,24},{24,28},{28,0},{1,5},{5... | collective-permute-start | bytes 1228808 | tf_op jit(solution)/shard_map/while/body/eval_jaxpr/ppermute | solution.py:73
  408.1 18.8 %collective-permute-start.1 = (bf16[160,1280]{1,0:T(8,128)(2,1)}, bf16[160,1280]{1,0:T(8,128)(2,1)}, u32[]{:S(2)}, u32[]{:S(2)}) collective-permute-start(bf16[160,1280]{1,0:T(8,128)(2,1)} %get-tuple-element.211), channel_id=1, source_target_pairs={{0,28},{4,0},{8,4},{12,8},{16,12},{20,16},{24,20},{28,24},{1,29},{... | collective-permute-start | bytes 1228808 | tf_op jit(solution)/shard_map/while/body/eval_jaxpr/ppermute | solution.py:80
  424.4 19.0 %collective-permute-start.2 = (bf16[160,1280]{1,0:T(8,128)(2,1)}, bf16[160,1280]{1,0:T(8,128)(2,1)S(1)}, u32[]{:S(2)}, u32[]{:S(2)}) collective-permute-start(bf16[160,1280]{1,0:T(8,128)(2,1)} %collective-permute-done), channel_id=1, source_target_pairs={{0,4},{4,8},{8,12},{12,16},{16,20},{20,24},{24,28},{28,0},{1,5},{5... | collective-permute-start | bytes 1228808 | tf_op jit(solution)/shard_map/while/body/eval_jaxpr/ppermute | solution.py:73
  426.9 18.9 %collective-permute-start.3 = (bf16[160,1280]{1,0:T(8,128)(2,1)}, bf16[160,1280]{1,0:T(8,128)(2,1)S(1)}, u32[]{:S(2)}, u32[]{:S(2)}) collective-permute-start(bf16[160,1280]{1,0:T(8,128)(2,1)} %collective-permute-done.1), channel_id=1, source_target_pairs={{0,28},{4,0},{8,4},{12,8},{16,12},{20,16},{24,20},{28,24},{1,29},{... | collective-permute-start | bytes 1228808 | tf_op jit(solution)/shard_map/while/body/eval_jaxpr/ppermute | solution.py:80
  443.4 18.6 %collective-permute-start.4 = (bf16[160,1280]{1,0:T(8,128)(2,1)S(1)}, bf16[160,1280]{1,0:T(8,128)(2,1)S(1)}, u32[]{:S(2)}, u32[]{:S(2)}) collective-permute-start(bf16[160,1280]{1,0:T(8,128)(2,1)S(1)} %collective-permute-done.2), channel_id=1, source_target_pairs={{0,4},{4,8},{8,12},{12,16},{16,20},{20,24},{24,28},{28,0},{1,5},{5... | collective-permute-start | bytes 1228808 | tf_op jit(solution)/shard_map/while/body/eval_jaxpr/ppermute | solution.py:73
  445.8 19.0 %collective-permute-start.5 = (bf16[160,1280]{1,0:T(8,128)(2,1)S(1)}, bf16[160,1280]{1,0:T(8,128)(2,1)S(1)}, u32[]{:S(2)}, u32[]{:S(2)}) collective-permute-start(bf16[160,1280]{1,0:T(8,128)(2,1)S(1)} %collective-permute-done.3), channel_id=1, source_target_pairs={{0,28},{4,0},{8,4},{12,8},{16,12},{20,16},{24,20},{28,24},{1,29},{... | collective-permute-start | bytes 1228808 | tf_op jit(solution)/shard_map/while/body/eval_jaxpr/ppermute | solution.py:80
  462.0 12.8 %collective-permute-start.6 = (bf16[160,1280]{1,0:T(8,128)(2,1)S(1)}, bf16[160,1280]{1,0:T(8,128)(2,1)S(1)}, u32[]{:S(2)}, u32[]{:S(2)}) collective-permute-start(bf16[160,1280]{1,0:T(8,128)(2,1)S(1)} %collective-permute-done.4), channel_id=1, source_target_pairs={{0,4},{4,8},{8,12},{12,16},{16,20},{20,24},{24,28},{28,0},{1,5},{5... | collective-permute-start | bytes 1228808 | tf_op jit(solution)/shard_map/while/body/eval_jaxpr/ppermute | solution.py:73
  481.5 16.1 %collective-permute-start = (bf16[160,1280]{1,0:T(8,128)(2,1)}, bf16[160,1280]{1,0:T(8,128)(2,1)}, u32[]{:S(2)}, u32[]{:S(2)}) collective-permute-start(bf16[160,1280]{1,0:T(8,128)(2,1)} %get-tuple-element.211), channel_id=1, source_target_pairs={{0,4},{4,8},{8,12},{12,16},{16,20},{20,24},{24,28},{28,0},{1,5},{5... | collective-permute-start | bytes 1228808 | tf_op jit(solution)/shard_map/while/body/eval_jaxpr/ppermute | solution.py:73
  481.5 18.6 %collective-permute-start.1 = (bf16[160,1280]{1,0:T(8,128)(2,1)}, bf16[160,1280]{1,0:T(8,128)(2,1)}, u32[]{:S(2)}, u32[]{:S(2)}) collective-permute-start(bf16[160,1280]{1,0:T(8,128)(2,1)} %get-tuple-element.211), channel_id=1, source_target_pairs={{0,28},{4,0},{8,4},{12,8},{16,12},{20,16},{24,20},{28,24},{1,29},{... | collective-permute-start | bytes 1228808 | tf_op jit(solution)/shard_map/while/body/eval_jaxpr/ppermute | solution.py:80
  497.6 18.8 %collective-permute-start.2 = (bf16[160,1280]{1,0:T(8,128)(2,1)}, bf16[160,1280]{1,0:T(8,128)(2,1)S(1)}, u32[]{:S(2)}, u32[]{:S(2)}) collective-permute-start(bf16[160,1280]{1,0:T(8,128)(2,1)} %collective-permute-done), channel_id=1, source_target_pairs={{0,4},{4,8},{8,12},{12,16},{16,20},{20,24},{24,28},{28,0},{1,5},{5... | collective-permute-start | bytes 1228808 | tf_op jit(solution)/shard_map/while/body/eval_jaxpr/ppermute | solution.py:73
  500.1 18.7 %collective-permute-start.3 = (bf16[160,1280]{1,0:T(8,128)(2,1)}, bf16[160,1280]{1,0:T(8,128)(2,1)S(1)}, u32[]{:S(2)}, u32[]{:S(2)}) collective-permute-start(bf16[160,1280]{1,0:T(8,128)(2,1)} %collective-permute-done.1), channel_id=1, source_target_pairs={{0,28},{4,0},{8,4},{12,8},{16,12},{20,16},{24,20},{28,24},{1,29},{... | collective-permute-start | bytes 1228808 | tf_op jit(solution)/shard_map/while/body/eval_jaxpr/ppermute | solution.py:80
  516.4 18.2 %collective-permute-start.4 = (bf16[160,1280]{1,0:T(8,128)(2,1)S(1)}, bf16[160,1280]{1,0:T(8,128)(2,1)S(1)}, u32[]{:S(2)}, u32[]{:S(2)}) collective-permute-start(bf16[160,1280]{1,0:T(8,128)(2,1)S(1)} %collective-permute-done.2), channel_id=1, source_target_pairs={{0,4},{4,8},{8,12},{12,16},{16,20},{20,24},{24,28},{28,0},{1,5},{5... | collective-permute-start | bytes 1228808 | tf_op jit(solution)/shard_map/while/body/eval_jaxpr/ppermute | solution.py:73
  518.8 20.0 %collective-permute-start.5 = (bf16[160,1280]{1,0:T(8,128)(2,1)S(1)}, bf16[160,1280]{1,0:T(8,128)(2,1)S(1)}, u32[]{:S(2)}, u32[]{:S(2)}) collective-permute-start(bf16[160,1280]{1,0:T(8,128)(2,1)S(1)} %collective-permute-done.3), channel_id=1, source_target_pairs={{0,28},{4,0},{8,4},{12,8},{16,12},{20,16},{24,20},{28,24},{1,29},{... | collective-permute-start | bytes 1228808 | tf_op jit(solution)/shard_map/while/body/eval_jaxpr/ppermute | solution.py:80
  534.7 12.5 %collective-permute-start.6 = (bf16[160,1280]{1,0:T(8,128)(2,1)S(1)}, bf16[160,1280]{1,0:T(8,128)(2,1)S(1)}, u32[]{:S(2)}, u32[]{:S(2)}) collective-permute-start(bf16[160,1280]{1,0:T(8,128)(2,1)S(1)} %collective-permute-done.4), channel_id=1, source_target_pairs={{0,4},{4,8},{8,12},{12,16},{16,20},{20,24},{24,28},{28,0},{1,5},{5... | collective-permute-start | bytes 1228808 | tf_op jit(solution)/shard_map/while/body/eval_jaxpr/ppermute | solution.py:73
  553.8 15.8 %collective-permute-start = (bf16[160,1280]{1,0:T(8,128)(2,1)}, bf16[160,1280]{1,0:T(8,128)(2,1)}, u32[]{:S(2)}, u32[]{:S(2)}) collective-permute-start(bf16[160,1280]{1,0:T(8,128)(2,1)} %get-tuple-element.211), channel_id=1, source_target_pairs={{0,4},{4,8},{8,12},{12,16},{16,20},{20,24},{24,28},{28,0},{1,5},{5... | collective-permute-start | bytes 1228808 | tf_op jit(solution)/shard_map/while/body/eval_jaxpr/ppermute | solution.py:73
  553.8 18.2 %collective-permute-start.1 = (bf16[160,1280]{1,0:T(8,128)(2,1)}, bf16[160,1280]{1,0:T(8,128)(2,1)}, u32[]{:S(2)}, u32[]{:S(2)}) collective-permute-start(bf16[160,1280]{1,0:T(8,128)(2,1)} %get-tuple-element.211), channel_id=1, source_target_pairs={{0,28},{4,0},{8,4},{12,8},{16,12},{20,16},{24,20},{28,24},{1,29},{... | collective-permute-start | bytes 1228808 | tf_op jit(solution)/shard_map/while/body/eval_jaxpr/ppermute | solution.py:80
  569.6 18.8 %collective-permute-start.2 = (bf16[160,1280]{1,0:T(8,128)(2,1)}, bf16[160,1280]{1,0:T(8,128)(2,1)S(1)}, u32[]{:S(2)}, u32[]{:S(2)}) collective-permute-start(bf16[160,1280]{1,0:T(8,128)(2,1)} %collective-permute-done), channel_id=1, source_target_pairs={{0,4},{4,8},{8,12},{12,16},{16,20},{20,24},{24,28},{28,0},{1,5},{5... | collective-permute-start | bytes 1228808 | tf_op jit(solution)/shard_map/while/body/eval_jaxpr/ppermute | solution.py:73
  572.1 18.7 %collective-permute-start.3 = (bf16[160,1280]{1,0:T(8,128)(2,1)}, bf16[160,1280]{1,0:T(8,128)(2,1)S(1)}, u32[]{:S(2)}, u32[]{:S(2)}) collective-permute-start(bf16[160,1280]{1,0:T(8,128)(2,1)} %collective-permute-done.1), channel_id=1, source_target_pairs={{0,28},{4,0},{8,4},{12,8},{16,12},{20,16},{24,20},{28,24},{1,29},{... | collective-permute-start | bytes 1228808 | tf_op jit(solution)/shard_map/while/body/eval_jaxpr/ppermute | solution.py:80
  588.4 18.2 %collective-permute-start.4 = (bf16[160,1280]{1,0:T(8,128)(2,1)S(1)}, bf16[160,1280]{1,0:T(8,128)(2,1)S(1)}, u32[]{:S(2)}, u32[]{:S(2)}) collective-permute-start(bf16[160,1280]{1,0:T(8,128)(2,1)S(1)} %collective-permute-done.2), channel_id=1, source_target_pairs={{0,4},{4,8},{8,12},{12,16},{16,20},{20,24},{24,28},{28,0},{1,5},{5... | collective-permute-start | bytes 1228808 | tf_op jit(solution)/shard_map/while/body/eval_jaxpr/ppermute | solution.py:73
  590.8 18.4 %collective-permute-start.5 = (bf16[160,1280]{1,0:T(8,128)(2,1)S(1)}, bf16[160,1280]{1,0:T(8,128)(2,1)S(1)}, u32[]{:S(2)}, u32[]{:S(2)}) collective-permute-start(bf16[160,1280]{1,0:T(8,128)(2,1)S(1)} %collective-permute-done.3), channel_id=1, source_target_pairs={{0,28},{4,0},{8,4},{12,8},{16,12},{20,16},{24,20},{28,24},{1,29},{... | collective-permute-start | bytes 1228808 | tf_op jit(solution)/shard_map/while/body/eval_jaxpr/ppermute | solution.py:80
  606.6 15.5 %collective-permute-start.6 = (bf16[160,1280]{1,0:T(8,128)(2,1)S(1)}, bf16[160,1280]{1,0:T(8,128)(2,1)S(1)}, u32[]{:S(2)}, u32[]{:S(2)}) collective-permute-start(bf16[160,1280]{1,0:T(8,128)(2,1)S(1)} %collective-permute-done.4), channel_id=1, source_target_pairs={{0,4},{4,8},{8,12},{12,16},{16,20},{20,24},{24,28},{28,0},{1,5},{5... | collective-permute-start | bytes 1228808 | tf_op jit(solution)/shard_map/while/body/eval_jaxpr/ppermute | solution.py:73
  628.8 13.7 %collective-permute-start = (bf16[160,1280]{1,0:T(8,128)(2,1)}, bf16[160,1280]{1,0:T(8,128)(2,1)}, u32[]{:S(2)}, u32[]{:S(2)}) collective-permute-start(bf16[160,1280]{1,0:T(8,128)(2,1)} %get-tuple-element.211), channel_id=1, source_target_pairs={{0,4},{4,8},{8,12},{12,16},{16,20},{20,24},{24,28},{28,0},{1,5},{5... | collective-permute-start | bytes 1228808 | tf_op jit(solution)/shard_map/while/body/eval_jaxpr/ppermute | solution.py:73
  628.8 16.1 %collective-permute-start.1 = (bf16[160,1280]{1,0:T(8,128)(2,1)}, bf16[160,1280]{1,0:T(8,128)(2,1)}, u32[]{:S(2)}, u32[]{:S(2)}) collective-permute-start(bf16[160,1280]{1,0:T(8,128)(2,1)} %get-tuple-element.211), channel_id=1, source_target_pairs={{0,28},{4,0},{8,4},{12,8},{16,12},{20,16},{24,20},{28,24},{1,29},{... | collective-permute-start | bytes 1228808 | tf_op jit(solution)/shard_map/while/body/eval_jaxpr/ppermute | solution.py:80
  642.4 19.2 %collective-permute-start.2 = (bf16[160,1280]{1,0:T(8,128)(2,1)}, bf16[160,1280]{1,0:T(8,128)(2,1)S(1)}, u32[]{:S(2)}, u32[]{:S(2)}) collective-permute-start(bf16[160,1280]{1,0:T(8,128)(2,1)} %collective-permute-done), channel_id=1, source_target_pairs={{0,4},{4,8},{8,12},{12,16},{16,20},{20,24},{24,28},{28,0},{1,5},{5... | collective-permute-start | bytes 1228808 | tf_op jit(solution)/shard_map/while/body/eval_jaxpr/ppermute | solution.py:73
  644.9 19.1 %collective-permute-start.3 = (bf16[160,1280]{1,0:T(8,128)(2,1)}, bf16[160,1280]{1,0:T(8,128)(2,1)S(1)}, u32[]{:S(2)}, u32[]{:S(2)}) collective-permute-start(bf16[160,1280]{1,0:T(8,128)(2,1)} %collective-permute-done.1), channel_id=1, source_target_pairs={{0,28},{4,0},{8,4},{12,8},{16,12},{20,16},{24,20},{28,24},{1,29},{... | collective-permute-start | bytes 1228808 | tf_op jit(solution)/shard_map/while/body/eval_jaxpr/ppermute | solution.py:80
  661.6 19.0 %collective-permute-start.4 = (bf16[160,1280]{1,0:T(8,128)(2,1)S(1)}, bf16[160,1280]{1,0:T(8,128)(2,1)S(1)}, u32[]{:S(2)}, u32[]{:S(2)}) collective-permute-start(bf16[160,1280]{1,0:T(8,128)(2,1)S(1)} %collective-permute-done.2), channel_id=1, source_target_pairs={{0,4},{4,8},{8,12},{12,16},{16,20},{20,24},{24,28},{28,0},{1,5},{5... | collective-permute-start | bytes 1228808 | tf_op jit(solution)/shard_map/while/body/eval_jaxpr/ppermute | solution.py:73
  664.0 19.1 %collective-permute-start.5 = (bf16[160,1280]{1,0:T(8,128)(2,1)S(1)}, bf16[160,1280]{1,0:T(8,128)(2,1)S(1)}, u32[]{:S(2)}, u32[]{:S(2)}) collective-permute-start(bf16[160,1280]{1,0:T(8,128)(2,1)S(1)} %collective-permute-done.3), channel_id=1, source_target_pairs={{0,28},{4,0},{8,4},{12,8},{16,12},{20,16},{24,20},{28,24},{1,29},{... | collective-permute-start | bytes 1228808 | tf_op jit(solution)/shard_map/while/body/eval_jaxpr/ppermute | solution.py:80
  680.6 13.1 %collective-permute-start.6 = (bf16[160,1280]{1,0:T(8,128)(2,1)S(1)}, bf16[160,1280]{1,0:T(8,128)(2,1)S(1)}, u32[]{:S(2)}, u32[]{:S(2)}) collective-permute-start(bf16[160,1280]{1,0:T(8,128)(2,1)S(1)} %collective-permute-done.4), channel_id=1, source_target_pairs={{0,4},{4,8},{8,12},{12,16},{16,20},{20,24},{24,28},{28,0},{1,5},{5... | collective-permute-start | bytes 1228808 | tf_op jit(solution)/shard_map/while/body/eval_jaxpr/ppermute | solution.py:73
  (23 other events, 1133.3 us)
